TPU v7x, 256 devices: a whole 4x4x8 slice. The times are simulated.
256 devices in a mesh: rep: 16 (over x, z_lo, core), fsdp: 16 (over y, z_hi).
Axes of the slice: x: 4, y: 4, z: 8 (z_hi: 4, z_lo: 2; z = z_hi * 2 + z_lo), core: 2. Of those that a mesh axis runs over, the one named last changes fastest.
Arguments:
- grad_gate: float32 [16, 128, 28672], P('rep', None, 'fsdp'), may hold values from -50 to 50
- grad_down: float32 [16, 256, 8192], P('rep', None, 'fsdp'), may hold values from -50 to 50
- param_gate: float32 [128, 28672], P(None, 'fsdp'), may hold values from -6 to 6
- mom1_gate: float32 [128, 28672], P(None, 'fsdp'), may hold values from -3 to 3
- mom2_gate: float32 [128, 28672], P(None, 'fsdp'), may hold values from 0.1 to 1
- param_down: float32 [256, 8192], P(None, 'fsdp'), may hold values from -6 to 6
- mom1_down: float32 [256, 8192], P(None, 'fsdp'), may hold values from -3 to 3
- mom2_down: float32 [256, 8192], P(None, 'fsdp'), may hold values from 0.1 to 1
Outputs:
- combined_gate: float32 [128, 28672], P(None, 'fsdp')
- new_param_gate: float32 [128, 28672], P(None, 'fsdp')
- new_mom1_gate: float32 [128, 28672], P(None, 'fsdp')
- new_mom2_gate: float32 [128, 28672], P(None, 'fsdp')
- combined_down: float32 [256, 8192], P(None, 'fsdp')
- new_param_down: float32 [256, 8192], P(None, 'fsdp')
- new_mom1_down: float32 [256, 8192], P(None, 'fsdp')
- new_mom2_down: float32 [256, 8192], P(None, 'fsdp')
All inputs are finite; a program needn't handle non-finite values.
Results may differ from a plain program's by a relative error of at most 0.0001.
Values sent between devices are 32-bit elements; how exact they have to be, the bound alone decides.
A program may use at most 64 MiB of HBM per device.

v0:
```python
import jax
import jax.numpy as jnp
from jax import lax
from jax.sharding import PartitionSpec as P


def swapped(x, axis, bit):
    return lax.ppermute(x, axis, [(i, i ^ 1 << bit) for i in range(lax.axis_size(axis))])


def adamw_rows(gradient, weights, moment_one, moment_two):
    new_one = 0.9 * moment_one + 0.1 * gradient
    new_two = 0.95 * moment_two + 0.05 * gradient * gradient
    corrected_one = new_one / (1.0 - 0.9**10)
    corrected_two = new_two / (1.0 - 0.95**10)
    step_size = corrected_one / (jnp.sqrt(corrected_two) + 1e-08) + 0.1 * weights
    return (weights - 0.05 * step_size, new_one, new_two)


def flip_sides(partials):
    return jnp.stack([partials[:, 0], partials[:, 2], partials[:, 1]], axis=1)


def group_sums(partials, level_bit, levels):
    running = lax.psum(partials, "fsdp")
    for upper_bit in range(level_bit, levels):
        received = swapped(running, "rep", upper_bit)
        if upper_bit == level_bit:
            received = flip_sides(received)
        running = running + received
    return running


def local(grad_gate, grad_down, param_gate, mom1_gate, mom2_gate, param_down, mom1_down, mom2_down):
    replicas = lax.axis_size("rep")
    levels = replicas.bit_length() - 1
    rep_index = lax.axis_index("rep")
    holdings = (grad_gate[0], grad_down[0])
    for step_level in range(levels):
        level_bit = levels - 1 - step_level
        upper_half = rep_index // (1 << level_bit) % 2
        retained = []
        outgoing = []
        for tensor in holdings:
            half_rows = tensor.shape[0] // 2
            retained.append(lax.dynamic_slice_in_dim(tensor, upper_half * half_rows, half_rows, 0))
            outgoing.append(
                lax.dynamic_slice_in_dim(tensor, (1 - upper_half) * half_rows, half_rows, 0)
            )
        incoming = swapped((outgoing[0], outgoing[1]), "rep", level_bit)
        rows_list = []
        for mine_part, their_part in zip(retained, incoming):
            rows_list.append(
                jnp.stack(
                    [
                        jnp.sum(mine_part * their_part),
                        jnp.sum(mine_part * mine_part),
                        jnp.sum(their_part * their_part),
                    ]
                )
            )
        partials = jnp.stack(rows_list)
        totals = group_sums(partials, level_bit, levels)
        merged = []
        for number in range(2):
            own_coef = 1.0 - totals[number, 0] / (2.0 * totals[number, 1])
            their_coef = 1.0 - totals[number, 0] / (2.0 * totals[number, 2])
            merged.append(own_coef * retained[number] + their_coef * incoming[number])
        holdings = (merged[0], merged[1])
    full_gate, full_down = (
        lax.all_gather(holdings[0], "rep", axis=0, tiled=True),
        lax.all_gather(holdings[1], "rep", axis=0, tiled=True),
    )
    gate_param, gate_one, gate_two = adamw_rows(full_gate, param_gate, mom1_gate, mom2_gate)
    down_param, down_one, down_two = adamw_rows(full_down, param_down, mom1_down, mom2_down)
    return (full_gate, gate_param, gate_one, gate_two, full_down, down_param, down_one, down_two)


def solution(mesh):
    in_specs = (
        P("rep", None, "fsdp"),
        P("rep", None, "fsdp"),
        P(None, "fsdp"),
        P(None, "fsdp"),
        P(None, "fsdp"),
        P(None, "fsdp"),
        P(None, "fsdp"),
        P(None, "fsdp"),
    )
    out_specs = (
        P(None, "fsdp"),
        P(None, "fsdp"),
        P(None, "fsdp"),
        P(None, "fsdp"),
        P(None, "fsdp"),
        P(None, "fsdp"),
        P(None, "fsdp"),
        P(None, "fsdp"),
    )
    return jax.shard_map(local, mesh=mesh, in_specs=in_specs, out_specs=out_specs, check_vma=False)
```

profile of v0, /device:TPU:1, one launch (start us, length us, event | category | flops | bytes accessed | tf_op | source)
XLA Modules:
  0.0 335.4 jit_solution(10442617677239891884)
XLA Ops:
  0.7 1.2 dynamic-slice_bitcast_fusion
  1.8 3.7 %collective-permute-start = (f32[64,1792]{1,0:T(8,128)S(1)}, f32[64,1792]{1,0:T(8,128)S(1)}, u32[]{:S(2)}, u32[]{:S(2)}) collective-permute-start(f32[64,1792]{1,0:T(8,128)S(1)} %dynamic-slice_bitcast_fusion), channel_id=1, source_target_pairs={{0,128},{16,144},{32,160},{48,176},{64,192},{80,208},{96,224},{112... | collective-permute-start | bytes 1376264 | tf_op jit(solution)/shard_map/ppermute | solution.py:8
  5.8 14.6 %collective-permute-done.1 = f32[128,512]{1,0:T(8,128)S(1)} collective-permute-done((f32[128,512]{1,0:T(8,128)S(1)}, f32[128,512]{1,0:T(8,128)S(1)}, u32[]{:S(2)}, u32[]{:S(2)}) %collective-permute-start.1) | collective-permute-done | bytes 262176 | tf_op jit(solution)/shard_map/ppermute | solution.py:8
  20.3 0.7 fusion.5
  21.0 0.7 fusion.2
  21.8 4.0 %maximum_bitcast_fusion = (f32[1,3]{1,0:T(1,128)S(1)}, f32[1,3]{1,0:T(1,128)S(1)}) fusion(f32[1]{0:T(128)} %bitcast.4, f32[1]{0:T(128)} %bitcast.3, f32[1]{0:T(128)} %bitcast.2, f32[1]{0:T(128)} %bitcast.10, f32[1]{0:T(128)} %bitcast.9, f32[1]{0:T(128)} %bitcast.8), kind=kLoop, calls=%fused_computation.62 | loop fusion | flops 12 | bytes 48 | tf_op jit(solution)/shard_map/stack | solution.py:62
  25.7 41.8 %psum.28 = f32[2,3]{1,0:T(2,128)S(1)} all-reduce(f32[2,3]{1,0:T(2,128)S(1)} %pad_maximum_fusion), channel_id=1, replica_groups=mesh['rep'=16,'fsdp'=16] {'fsdp'}, use_global_device_ids=true, to_apply=%region_6.7 | all-reduce | flops 6 | bytes 48 | tf_op jit(solution)/shard_map/psum | solution.py:25
  67.5 2.8 collective-permute-start.2
  70.4 1.2 collective-permute-done.2
  77.6 1.3 collective-permute-start.4
  79.3 2.2 collective-permute-done.4
  82.1 2.0 maximum_bitcast_fusion.3
  84.8 2.0 maximum_bitcast_fusion.2
  86.9 32.1 %psum.29 = f32[2,3]{1,0:T(2,128)S(1)} all-reduce(f32[2,3]{1,0:T(2,128)S(1)} %pad_maximum_fusion.1), channel_id=1, replica_groups=mesh['rep'=16,'fsdp'=16] {'fsdp'}, use_global_device_ids=true, to_apply=%region_13.14 | all-reduce | flops 6 | bytes 48 | tf_op jit(solution)/shard_map/psum | solution.py:25
  119.0 1.3 collective-permute-start.5
  120.3 1.5 collective-permute-done.5
  121.9 2.8 collective-permute-start.6
  124.7 1.4 collective-permute-done.6
  132.1 0.8 collective-permute-start.8
  132.9 0.8 collective-permute-start.7
  133.8 1.8 collective-permute-done.8
  136.2 2.0 maximum_bitcast_fusion.5
  138.9 2.0 maximum_bitcast_fusion.4
  140.9 33.9 %psum.30 = f32[2,3]{1,0:T(2,128)S(1)} all-reduce(f32[2,3]{1,0:T(2,128)S(1)} %pad_maximum_fusion.2), channel_id=1, replica_groups=mesh['rep'=16,'fsdp'=16] {'fsdp'}, use_global_device_ids=true, to_apply=%region_20.21 | all-reduce | flops 6 | bytes 48 | tf_op jit(solution)/shard_map/psum | solution.py:25
  174.8 0.9 collective-permute-start.9
  175.6 1.9 collective-permute-done.9
  177.7 1.2 collective-permute-start.10
  178.9 1.5 collective-permute-done.10
  180.5 2.7 collective-permute-start.11
  183.3 1.2 collective-permute-done.11
  190.3 31.6 %collective-permute-start.13 = (f32[16,512]{1,0:T(8,128)S(1)}, f32[16,512]{1,0:T(8,128)S(1)}, u32[]{:S(2)}, u32[]{:S(2)}) collective-permute-start(f32[16,512]{1,0:T(8,128)S(1)} %constant_dynamic-slice_fusion), channel_id=1, source_target_pairs={{0,16},{16,0},{32,48},{48,32},{64,80},{80,64},{96,112},{112,96},{1... | collective-permute-start | bytes 98312 | tf_op jit(solution)/shard_map/ppermute | solution.py:8
  222.1 0.7 collective-permute-done.13
  223.4 2.0 maximum_bitcast_fusion.7
  226.1 2.0 maximum_bitcast_fusion.6
  228.1 32.2 %psum.31 = f32[2,3]{1,0:T(2,128)S(1)} all-reduce(f32[2,3]{1,0:T(2,128)S(1)} %pad_maximum_fusion.3), channel_id=1, replica_groups=mesh['rep'=16,'fsdp'=16] {'fsdp'}, use_global_device_ids=true, to_apply=%region_27.28 | all-reduce | flops 6 | bytes 48 | tf_op jit(solution)/shard_map/psum | solution.py:25
  260.3 7.3 %collective-permute-start.14 = (f32[2,3]{1,0:T(2,128)S(1)}, f32[2,3]{1,0:T(2,128)S(1)}, u32[]{:S(2)}, u32[]{:S(2)}) collective-permute-start(f32[2,3]{1,0:T(2,128)S(1)} %psum.31), channel_id=1, source_target_pairs={{0,16},{16,0},{32,48},{48,32},{64,80},{80,64},{96,112},{112,96},{1... | collective-permute-start | bytes 80 | tf_op jit(solution)/shard_map/ppermute | solution.py:8
  267.6 0.8 collective-permute-done.14
  269.2 1.8 collective-permute-done.15
  271.1 1.1 collective-permute-start.16
  272.2 1.3 collective-permute-done.16
  273.5 2.6 collective-permute-start.17
  276.1 1.3 collective-permute-done.17
  283.3 25.1 %all_gather.7 = f32[256,512]{1,0:T(8,128)S(1)} all-gather(f32[16,512]{1,0:T(8,128)S(1)} %multiply_add_fusion.7), channel_id=1, replica_groups=mesh['rep'=16,'fsdp'=16] {'rep'}, dimensions={0}, use_global_device_ids=true | all-gather | bytes 557056 | tf_op jit(solution)/shard_map/all_gather | solution.py:72
  308.4 21.0 %all_gather.6 = f32[128,1792]{1,0:T(8,128)S(1)} all-gather(f32[8,1792]{1,0:T(8,128)S(1)} %multiply_add_fusion.6), channel_id=1, replica_groups=mesh['rep'=16,'fsdp'=16] {'rep'}, dimensions={0}, use_global_device_ids=true | all-gather | bytes 974848 | tf_op jit(solution)/shard_map/all_gather | solution.py:71
  329.5 1.4 multiply_subtract_fusion.1
  331.7 2.0 multiply_subtract_fusion
  333.7 0.9 copy.18
  334.6 0.8 copy.19
  (67 shorter events, 9.6 us)
Async XLA Ops:
  0.6 4.9 %copy-start.1 = (f32[1,256,512]{2,1,0:T(8,128)S(1)}, f32[1,256,512]{2,1,0:T(8,128)}, u32[]{:S(2)}) copy-start(f32[1,256,512]{2,1,0:T(8,128)} %param.9) | copy-start | bytes 1572868
  0.7 20.3 %copy-start = (f32[1,128,1792]{2,1,0:T(8,128)S(1)}, f32[1,128,1792]{2,1,0:T(8,128)}, u32[]{:S(2)}) copy-start(f32[1,128,1792]{2,1,0:T(8,128)} %param.8) | copy-start | bytes 2752516
  1.8 19.2 %collective-permute-start = (f32[64,1792]{1,0:T(8,128)S(1)}, f32[64,1792]{1,0:T(8,128)S(1)}, u32[]{:S(2)}, u32[]{:S(2)}) collective-permute-start(f32[64,1792]{1,0:T(8,128)S(1)} %dynamic-slice_bitcast_fusion), channel_id=1, source_target_pairs={{0,128},{16,144},{32,160},{48,176},{64,192},{80,208},{96,224},{112... | collective-permute-start | bytes 1376264 | tf_op jit(solution)/shard_map/ppermute | solution.py:8
  5.5 14.8 %collective-permute-start.1 = (f32[128,512]{1,0:T(8,128)S(1)}, f32[128,512]{1,0:T(8,128)S(1)}, u32[]{:S(2)}, u32[]{:S(2)}) collective-permute-start(f32[128,512]{1,0:T(8,128)S(1)} %dynamic-slice_bitcast_fusion.1), channel_id=1, source_target_pairs={{0,128},{16,144},{32,160},{48,176},{64,192},{80,208},{96,224},{112... | collective-permute-start | bytes 786440 | tf_op jit(solution)/shard_map/ppermute | solution.py:8
  67.5 4.0 %collective-permute-start.2 = (f32[2,3]{1,0:T(2,128)S(1)}, f32[2,3]{1,0:T(2,128)S(1)}, u32[]{:S(2)}, u32[]{:S(2)}) collective-permute-start(f32[2,3]{1,0:T(2,128)S(1)} %psum.28), channel_id=1, source_target_pairs={{0,128},{16,144},{32,160},{48,176},{64,192},{80,208},{96,224},{112... | collective-permute-start | bytes 80 | tf_op jit(solution)/shard_map/ppermute | solution.py:8
  77.6 3.9 %collective-permute-start.4 = (f32[64,512]{1,0:T(8,128)S(1)}, f32[64,512]{1,0:T(8,128)S(1)}, u32[]{:S(2)}, u32[]{:S(2)}) collective-permute-start(f32[64,512]{1,0:T(8,128)S(1)} %constant_dynamic-slice_fusion.4), channel_id=1, source_target_pairs={{0,64},{16,80},{32,96},{48,112},{64,0},{80,16},{96,32},{112,48},{1... | collective-permute-start | bytes 393224 | tf_op jit(solution)/shard_map/ppermute | solution.py:8
  79.0 5.2 %collective-permute-start.3 = (f32[32,1792]{1,0:T(8,128)S(1)}, f32[32,1792]{1,0:T(8,128)S(1)}, u32[]{:S(2)}, u32[]{:S(2)}) collective-permute-start(f32[32,1792]{1,0:T(8,128)S(1)} %constant_dynamic-slice_fusion.5), channel_id=1, source_target_pairs={{0,64},{16,80},{32,96},{48,112},{64,0},{80,16},{96,32},{112,48},{1... | collective-permute-start | bytes 688136 | tf_op jit(solution)/shard_map/ppermute | solution.py:8
  119.0 2.8 collective-permute-start.5
  121.9 4.2 %collective-permute-start.6 = (f32[2,3]{1,0:T(2,128)S(1)}, f32[2,3]{1,0:T(2,128)S(1)}, u32[]{:S(2)}, u32[]{:S(2)}) collective-permute-start(f32[2,3]{1,0:T(2,128)S(1)} %maximum_add_fusion.1), channel_id=1, source_target_pairs={{0,128},{16,144},{32,160},{48,176},{64,192},{80,208},{96,224},{112... | collective-permute-start | bytes 80 | tf_op jit(solution)/shard_map/ppermute | solution.py:8
  132.1 3.5 %collective-permute-start.8 = (f32[32,512]{1,0:T(8,128)S(1)}, f32[32,512]{1,0:T(8,128)S(1)}, u32[]{:S(2)}, u32[]{:S(2)}) collective-permute-start(f32[32,512]{1,0:T(8,128)S(1)} %constant_dynamic-slice_fusion.2), channel_id=1, source_target_pairs={{0,32},{16,48},{32,0},{48,16},{64,96},{80,112},{96,64},{112,80},{1... | collective-permute-start | bytes 196616 | tf_op jit(solution)/shard_map/ppermute | solution.py:8
  132.9 5.3 %collective-permute-start.7 = (f32[16,1792]{1,0:T(8,128)S(1)}, f32[16,1792]{1,0:T(8,128)S(1)}, u32[]{:S(2)}, u32[]{:S(2)}) collective-permute-start(f32[16,1792]{1,0:T(8,128)S(1)} %constant_dynamic-slice_fusion.3), channel_id=1, source_target_pairs={{0,32},{16,48},{32,0},{48,16},{64,96},{80,112},{96,64},{112,80},{1... | collective-permute-start | bytes 344072 | tf_op jit(solution)/shard_map/ppermute | solution.py:8
  174.8 2.8 collective-permute-start.9
  177.7 2.7 collective-permute-start.10
  180.5 3.9 %collective-permute-start.11 = (f32[2,3]{1,0:T(2,128)S(1)}, f32[2,3]{1,0:T(2,128)S(1)}, u32[]{:S(2)}, u32[]{:S(2)}) collective-permute-start(f32[2,3]{1,0:T(2,128)S(1)} %fusion.19), channel_id=1, source_target_pairs={{0,128},{16,144},{32,160},{48,176},{64,192},{80,208},{96,224},{112... | collective-permute-start | bytes 80 | tf_op jit(solution)/shard_map/ppermute | solution.py:8
  190.3 32.5 %collective-permute-start.13 = (f32[16,512]{1,0:T(8,128)S(1)}, f32[16,512]{1,0:T(8,128)S(1)}, u32[]{:S(2)}, u32[]{:S(2)}) collective-permute-start(f32[16,512]{1,0:T(8,128)S(1)} %constant_dynamic-slice_fusion), channel_id=1, source_target_pairs={{0,16},{16,0},{32,48},{48,32},{64,80},{80,64},{96,112},{112,96},{1... | collective-permute-start | bytes 98312 | tf_op jit(solution)/shard_map/ppermute | solution.py:8
  222.0 3.5 %collective-permute-start.12 = (f32[8,1792]{1,0:T(8,128)S(1)}, f32[8,1792]{1,0:T(8,128)S(1)}, u32[]{:S(2)}, u32[]{:S(2)}) collective-permute-start(f32[8,1792]{1,0:T(8,128)S(1)} %constant_dynamic-slice_fusion.1), channel_id=1, source_target_pairs={{0,16},{16,0},{32,48},{48,32},{64,80},{80,64},{96,112},{112,96},{1... | collective-permute-start | bytes 172040 | tf_op jit(solution)/shard_map/ppermute | solution.py:8
  260.3 8.1 %collective-permute-start.14 = (f32[2,3]{1,0:T(2,128)S(1)}, f32[2,3]{1,0:T(2,128)S(1)}, u32[]{:S(2)}, u32[]{:S(2)}) collective-permute-start(f32[2,3]{1,0:T(2,128)S(1)} %psum.31), channel_id=1, source_target_pairs={{0,16},{16,0},{32,48},{48,32},{64,80},{80,64},{96,112},{112,96},{1... | collective-permute-start | bytes 80 | tf_op jit(solution)/shard_map/ppermute | solution.py:8
  268.5 2.4 collective-permute-start.15
  271.1 2.4 collective-permute-start.16
  273.5 3.9 %collective-permute-start.17 = (f32[2,3]{1,0:T(2,128)S(1)}, f32[2,3]{1,0:T(2,128)S(1)}, u32[]{:S(2)}, u32[]{:S(2)}) collective-permute-start(f32[2,3]{1,0:T(2,128)S(1)} %add.191), channel_id=1, source_target_pairs={{0,128},{16,144},{32,160},{48,176},{64,192},{80,208},{96,224},{112... | collective-permute-start | bytes 80 | tf_op jit(solution)/shard_map/ppermute | solution.py:8
  283.3 46.1 %copy-start.7 = (f32[256,512]{1,0:T(8,128)S(1)}, f32[256,512]{1,0:T(8,128)}, u32[]{:S(2)}) copy-start(f32[256,512]{1,0:T(8,128)} %param.15) | copy-start | bytes 1572868
  308.3 21.1 %copy-start.6 = (f32[256,512]{1,0:T(8,128)S(1)}, f32[256,512]{1,0:T(8,128)}, u32[]{:S(2)}) copy-start(f32[256,512]{1,0:T(8,128)} %param.14) | copy-start | bytes 1572868
  308.4 21.1 %copy-start.5 = (f32[256,512]{1,0:T(8,128)S(1)}, f32[256,512]{1,0:T(8,128)}, u32[]{:S(2)}) copy-start(f32[256,512]{1,0:T(8,128)} %param.13) | copy-start | bytes 1572868
  329.4 1.5 copy-start.2
  329.4 2.0 copy-start.3
  329.5 2.3 copy-start.4
where the time goes:
time: 336 us; the launch traced here: 335 us
  blocking collectives  186 us (55%)
  starting transfers between devices  62.1 us (18%)
  waiting for transfers between devices  33.3 us (10%)
  other arithmetic  25.5 us (8%)
  between operations  21.8 us (6%)
  local copies, waits for them, and re-layouts  6.56 us (2%)
    psum x4, blocking collectives, group_sums(): running = lax.psum(partials, 'fsdp')  140 us
    ppermute x18, starting transfers between devices, swapped(): lax.ppermute(x, axis, [(i, i ^ 1 << bit) for i in range(lax.axis_size(axi...  62.1 us
    ppermute x18, waiting for transfers between devices, swapped(): lax.ppermute(x, axis, [(i, i ^ 1 << bit) for i in range(lax.axis_size(axi...  33.3 us
    all_gather x1, blocking collectives, local(): lax.all_gather(holdings[1], 'rep', axis=0, tiled=True)  25.1 us
    all_gather x1, blocking collectives, local(): lax.all_gather(holdings[0], 'rep', axis=0, tiled=True)  21 us
    another operation x11, other arithmetic, local(): partials = jnp.stack(rows_list)  16.1 us
  transfers between devices with their start and end apart: 18, of which 14 were waited for; matrix products, arithmetic and copies ran while one was open for 3% of the time, Pallas kernels for 0%

commit v1 on v0

--- a/solution.py
+++ b/solution.py
@@ -22,7 +22,7 @@
 
 
 def group_sums(partials, level_bit, levels):
-    running = lax.psum(partials, "fsdp")
+    running = jnp.sum(lax.all_gather(partials, "fsdp"), axis=0)
     for upper_bit in range(level_bit, levels):
         received = swapped(running, "rep", upper_bit)
         if upper_bit == level_bit:

time: 336 us -> 332 us (0.988)
  blocking collectives: 186 us -> 182 us
    psum x4 -> x0, blocking collectives: 140 us -> none  [group_sums(): running = lax.psum(partials, 'fsdp')]
    all_gather x0 -> x4, blocking collectives: none -> 136 us  [group_sums(): running = jnp.sum(lax.all_gather(partials, 'fsdp'), axis=0)]
    another operation x11 -> x7, other arithmetic: 16.1 us -> 16 us  [local(): partials = jnp.stack(rows_list)]
where the time goes in v1:
time: 332 us; the launch traced here: 331 us
  blocking collectives  182 us (55%)
  starting transfers between devices  62.6 us (19%)
  waiting for transfers between devices  32.5 us (10%)
  other arithmetic  25.6 us (8%)
  between operations  21.8 us (7%)
  local copies, waits for them, and re-layouts  6.56 us (2%)
    all_gather x4, blocking collectives, group_sums(): running = jnp.sum(lax.all_gather(partials, 'fsdp'), axis=0)  136 us
    ppermute x18, starting transfers between devices, swapped(): lax.ppermute(x, axis, [(i, i ^ 1 << bit) for i in range(lax.axis_size(axi...  62.6 us
    ppermute x18, waiting for transfers between devices, swapped(): lax.ppermute(x, axis, [(i, i ^ 1 << bit) for i in range(lax.axis_size(axi...  32.5 us
    all_gather x1, blocking collectives, local(): lax.all_gather(holdings[1], 'rep', axis=0, tiled=True)  25.1 us
    all_gather x1, blocking collectives, local(): lax.all_gather(holdings[0], 'rep', axis=0, tiled=True)  21 us
    another operation x7, other arithmetic, local(): partials = jnp.stack(rows_list)  16 us
  transfers between devices with their start and end apart: 18, of which 14 were waited for; matrix products, arithmetic and copies ran while one was open for 3% of the time, Pallas kernels for 0%

profile of v1, /device:TPU:1, one launch (start us, length us, event | category | flops | bytes accessed | tf_op | source)
XLA Modules:
  0.0 331.1 jit_solution(13756466380912688748)
XLA Ops:
  0.7 1.2 dynamic-slice_bitcast_fusion
  1.8 3.7 %collective-permute-start = (f32[64,1792]{1,0:T(8,128)S(1)}, f32[64,1792]{1,0:T(8,128)S(1)}, u32[]{:S(2)}, u32[]{:S(2)}) collective-permute-start(f32[64,1792]{1,0:T(8,128)S(1)} %dynamic-slice_bitcast_fusion), channel_id=1, source_target_pairs={{0,128},{16,144},{32,160},{48,176},{64,192},{80,208},{96,224},{112... | collective-permute-start | bytes 1376264 | tf_op jit(solution)/shard_map/ppermute | solution.py:8
  5.8 14.6 %collective-permute-done.1 = f32[128,512]{1,0:T(8,128)S(1)} collective-permute-done((f32[128,512]{1,0:T(8,128)S(1)}, f32[128,512]{1,0:T(8,128)S(1)}, u32[]{:S(2)}, u32[]{:S(2)}) %collective-permute-start.1) | collective-permute-done | bytes 262176 | tf_op jit(solution)/shard_map/ppermute | solution.py:8
  21.0 0.7 fusion.2
  21.8 4.0 %maximum_bitcast_fusion.4 = (f32[1,3]{1,0:T(1,128)S(1)}, f32[1,3]{1,0:T(1,128)S(1)}) fusion(f32[1]{0:T(128)} %bitcast.4, f32[1]{0:T(128)} %bitcast.3, f32[1]{0:T(128)} %bitcast.2, f32[1]{0:T(128)} %bitcast.10, f32[1]{0:T(128)} %bitcast.9, f32[1]{0:T(128)} %bitcast.8), kind=kLoop, calls=%fused_computation.62 | loop fusion | flops 12 | bytes 48 | tf_op jit(solution)/shard_map/stack | solution.py:62
  25.7 40.4 %all-gather.4 = f32[16,2,3]{2,1,0:T(2,128)S(1)} all-gather(f32[1,2,3]{2,1,0:T(2,128)S(1)} %maximum_bitcast_fusion), channel_id=2, replica_groups=mesh['rep'=16,'fsdp'=16] {'fsdp'}, dimensions={0}, use_global_device_ids=true | all-gather | bytes 408 | tf_op jit(solution)/shard_map/all_gather | solution.py:25
  66.2 2.8 collective-permute-start.2
  69.0 1.2 collective-permute-done.2
  76.2 1.3 collective-permute-start.4
  78.0 2.2 collective-permute-done.4
  80.8 2.0 maximum_bitcast_fusion.7
  83.5 2.0 maximum_bitcast_fusion.6
  85.5 31.0 %all-gather.5 = f32[16,2,3]{2,1,0:T(2,128)S(1)} all-gather(f32[1,2,3]{2,1,0:T(2,128)S(1)} %maximum_bitcast_fusion.1), channel_id=3, replica_groups=mesh['rep'=16,'fsdp'=16] {'fsdp'}, dimensions={0}, use_global_device_ids=true | all-gather | bytes 408 | tf_op jit(solution)/shard_map/all_gather | solution.py:25
  116.6 1.3 collective-permute-start.5
  117.9 1.2 collective-permute-done.5
  119.2 2.8 collective-permute-start.6
  122.0 1.4 collective-permute-done.6
  129.3 0.8 collective-permute-start.8
  130.2 0.8 collective-permute-start.7
  131.0 1.8 collective-permute-done.8
  133.4 2.0 maximum_bitcast_fusion.9
  136.1 2.0 maximum_bitcast_fusion.8
  138.1 33.2 %all-gather.6 = f32[16,2,3]{2,1,0:T(2,128)S(1)} all-gather(f32[1,2,3]{2,1,0:T(2,128)S(1)} %maximum_bitcast_fusion.2), channel_id=4, replica_groups=mesh['rep'=16,'fsdp'=16] {'fsdp'}, dimensions={0}, use_global_device_ids=true | all-gather | bytes 408 | tf_op jit(solution)/shard_map/all_gather | solution.py:25
  171.3 0.8 collective-permute-start.9
  172.1 1.7 collective-permute-done.9
  174.0 1.2 collective-permute-start.10
  175.2 1.3 collective-permute-done.10
  176.6 2.7 collective-permute-start.11
  179.3 1.5 collective-permute-done.11
  186.7 31.9 %collective-permute-start.13 = (f32[16,512]{1,0:T(8,128)S(1)}, f32[16,512]{1,0:T(8,128)S(1)}, u32[]{:S(2)}, u32[]{:S(2)}) collective-permute-start(f32[16,512]{1,0:T(8,128)S(1)} %constant_dynamic-slice_fusion), channel_id=1, source_target_pairs={{0,16},{16,0},{32,48},{48,32},{64,80},{80,64},{96,112},{112,96},{1... | collective-permute-start | bytes 98312 | tf_op jit(solution)/shard_map/ppermute | solution.py:8
  218.7 0.7 collective-permute-done.13
  220.1 2.0 maximum_bitcast_fusion.11
  222.7 2.0 maximum_bitcast_fusion.10
  224.7 31.2 %all-gather.7 = f32[16,2,3]{2,1,0:T(2,128)S(1)} all-gather(f32[1,2,3]{2,1,0:T(2,128)S(1)} %maximum_bitcast_fusion.3), channel_id=5, replica_groups=mesh['rep'=16,'fsdp'=16] {'fsdp'}, dimensions={0}, use_global_device_ids=true | all-gather | bytes 408 | tf_op jit(solution)/shard_map/all_gather | solution.py:25
  255.9 7.3 %collective-permute-start.14 = (f32[2,3]{1,0:T(2,128)S(1)}, f32[2,3]{1,0:T(2,128)S(1)}, u32[]{:S(2)}, u32[]{:S(2)}) collective-permute-start(f32[2,3]{1,0:T(2,128)S(1)} %reduce_sum.279), channel_id=1, source_target_pairs={{0,16},{16,0},{32,48},{48,32},{64,80},{80,64},{96,112},{112,96},{1... | collective-permute-start | bytes 80 | tf_op jit(solution)/shard_map/ppermute | solution.py:8
  263.2 0.8 collective-permute-done.14
  264.2 0.8 collective-permute-start.15
  264.9 1.7 collective-permute-done.15
  266.7 1.2 collective-permute-start.16
  267.9 1.3 collective-permute-done.16
  269.1 2.7 collective-permute-start.17
  271.8 1.2 collective-permute-done.17
  278.9 25.1 %all_gather.39 = f32[256,512]{1,0:T(8,128)S(1)} all-gather(f32[16,512]{1,0:T(8,128)S(1)} %multiply_add_fusion.7), channel_id=1, replica_groups=mesh['rep'=16,'fsdp'=16] {'rep'}, dimensions={0}, use_global_device_ids=true | all-gather | bytes 557056 | tf_op jit(solution)/shard_map/all_gather | solution.py:72
  304.1 21.0 %all_gather.38 = f32[128,1792]{1,0:T(8,128)S(1)} all-gather(f32[8,1792]{1,0:T(8,128)S(1)} %multiply_add_fusion.6), channel_id=1, replica_groups=mesh['rep'=16,'fsdp'=16] {'rep'}, dimensions={0}, use_global_device_ids=true | all-gather | bytes 974848 | tf_op jit(solution)/shard_map/all_gather | solution.py:71
  325.2 1.4 multiply_subtract_fusion.1
  327.4 2.0 multiply_subtract_fusion
  329.4 0.9 copy.18
  330.3 0.8 copy.19
  (71 shorter events, 9.7 us)
Async XLA Ops:
  0.6 4.9 %copy-start.1 = (f32[1,256,512]{2,1,0:T(8,128)S(1)}, f32[1,256,512]{2,1,0:T(8,128)}, u32[]{:S(2)}) copy-start(f32[1,256,512]{2,1,0:T(8,128)} %param.9) | copy-start | bytes 1572868
  0.7 20.3 %copy-start = (f32[1,128,1792]{2,1,0:T(8,128)S(1)}, f32[1,128,1792]{2,1,0:T(8,128)}, u32[]{:S(2)}) copy-start(f32[1,128,1792]{2,1,0:T(8,128)} %param.8) | copy-start | bytes 2752516
  1.8 19.2 %collective-permute-start = (f32[64,1792]{1,0:T(8,128)S(1)}, f32[64,1792]{1,0:T(8,128)S(1)}, u32[]{:S(2)}, u32[]{:S(2)}) collective-permute-start(f32[64,1792]{1,0:T(8,128)S(1)} %dynamic-slice_bitcast_fusion), channel_id=1, source_target_pairs={{0,128},{16,144},{32,160},{48,176},{64,192},{80,208},{96,224},{112... | collective-permute-start | bytes 1376264 | tf_op jit(solution)/shard_map/ppermute | solution.py:8
  5.5 14.8 %collective-permute-start.1 = (f32[128,512]{1,0:T(8,128)S(1)}, f32[128,512]{1,0:T(8,128)S(1)}, u32[]{:S(2)}, u32[]{:S(2)}) collective-permute-start(f32[128,512]{1,0:T(8,128)S(1)} %dynamic-slice_bitcast_fusion.1), channel_id=1, source_target_pairs={{0,128},{16,144},{32,160},{48,176},{64,192},{80,208},{96,224},{112... | collective-permute-start | bytes 786440 | tf_op jit(solution)/shard_map/ppermute | solution.py:8
  66.2 4.0 %collective-permute-start.2 = (f32[2,3]{1,0:T(2,128)S(1)}, f32[2,3]{1,0:T(2,128)S(1)}, u32[]{:S(2)}, u32[]{:S(2)}) collective-permute-start(f32[2,3]{1,0:T(2,128)S(1)} %reduce_sum.258), channel_id=1, source_target_pairs={{0,128},{16,144},{32,160},{48,176},{64,192},{80,208},{96,224},{112... | collective-permute-start | bytes 80 | tf_op jit(solution)/shard_map/ppermute | solution.py:8
  76.2 3.9 %collective-permute-start.4 = (f32[64,512]{1,0:T(8,128)S(1)}, f32[64,512]{1,0:T(8,128)S(1)}, u32[]{:S(2)}, u32[]{:S(2)}) collective-permute-start(f32[64,512]{1,0:T(8,128)S(1)} %constant_dynamic-slice_fusion.4), channel_id=1, source_target_pairs={{0,64},{16,80},{32,96},{48,112},{64,0},{80,16},{96,32},{112,48},{1... | collective-permute-start | bytes 393224 | tf_op jit(solution)/shard_map/ppermute | solution.py:8
  77.6 5.2 %collective-permute-start.3 = (f32[32,1792]{1,0:T(8,128)S(1)}, f32[32,1792]{1,0:T(8,128)S(1)}, u32[]{:S(2)}, u32[]{:S(2)}) collective-permute-start(f32[32,1792]{1,0:T(8,128)S(1)} %constant_dynamic-slice_fusion.5), channel_id=1, source_target_pairs={{0,64},{16,80},{32,96},{48,112},{64,0},{80,16},{96,32},{112,48},{1... | collective-permute-start | bytes 688136 | tf_op jit(solution)/shard_map/ppermute | solution.py:8
  116.6 2.5 collective-permute-start.5
  119.2 4.1 %collective-permute-start.6 = (f32[2,3]{1,0:T(2,128)S(1)}, f32[2,3]{1,0:T(2,128)S(1)}, u32[]{:S(2)}, u32[]{:S(2)}) collective-permute-start(f32[2,3]{1,0:T(2,128)S(1)} %maximum_add_fusion.1), channel_id=1, source_target_pairs={{0,128},{16,144},{32,160},{48,176},{64,192},{80,208},{96,224},{112... | collective-permute-start | bytes 80 | tf_op jit(solution)/shard_map/ppermute | solution.py:8
  129.3 3.5 %collective-permute-start.8 = (f32[32,512]{1,0:T(8,128)S(1)}, f32[32,512]{1,0:T(8,128)S(1)}, u32[]{:S(2)}, u32[]{:S(2)}) collective-permute-start(f32[32,512]{1,0:T(8,128)S(1)} %constant_dynamic-slice_fusion.2), channel_id=1, source_target_pairs={{0,32},{16,48},{32,0},{48,16},{64,96},{80,112},{96,64},{112,80},{1... | collective-permute-start | bytes 196616 | tf_op jit(solution)/shard_map/ppermute | solution.py:8
  130.2 5.3 %collective-permute-start.7 = (f32[16,1792]{1,0:T(8,128)S(1)}, f32[16,1792]{1,0:T(8,128)S(1)}, u32[]{:S(2)}, u32[]{:S(2)}) collective-permute-start(f32[16,1792]{1,0:T(8,128)S(1)} %constant_dynamic-slice_fusion.3), channel_id=1, source_target_pairs={{0,32},{16,48},{32,0},{48,16},{64,96},{80,112},{96,64},{112,80},{1... | collective-permute-start | bytes 344072 | tf_op jit(solution)/shard_map/ppermute | solution.py:8
  171.3 2.5 collective-permute-start.9
  174.0 2.6 collective-permute-start.10
  176.6 4.2 %collective-permute-start.11 = (f32[2,3]{1,0:T(2,128)S(1)}, f32[2,3]{1,0:T(2,128)S(1)}, u32[]{:S(2)}, u32[]{:S(2)}) collective-permute-start(f32[2,3]{1,0:T(2,128)S(1)} %fusion.19), channel_id=1, source_target_pairs={{0,128},{16,144},{32,160},{48,176},{64,192},{80,208},{96,224},{112... | collective-permute-start | bytes 80 | tf_op jit(solution)/shard_map/ppermute | solution.py:8
  186.7 32.7 %collective-permute-start.13 = (f32[16,512]{1,0:T(8,128)S(1)}, f32[16,512]{1,0:T(8,128)S(1)}, u32[]{:S(2)}, u32[]{:S(2)}) collective-permute-start(f32[16,512]{1,0:T(8,128)S(1)} %constant_dynamic-slice_fusion), channel_id=1, source_target_pairs={{0,16},{16,0},{32,48},{48,32},{64,80},{80,64},{96,112},{112,96},{1... | collective-permute-start | bytes 98312 | tf_op jit(solution)/shard_map/ppermute | solution.py:8
  218.6 3.5 %collective-permute-start.12 = (f32[8,1792]{1,0:T(8,128)S(1)}, f32[8,1792]{1,0:T(8,128)S(1)}, u32[]{:S(2)}, u32[]{:S(2)}) collective-permute-start(f32[8,1792]{1,0:T(8,128)S(1)} %constant_dynamic-slice_fusion.1), channel_id=1, source_target_pairs={{0,16},{16,0},{32,48},{48,32},{64,80},{80,64},{96,112},{112,96},{1... | collective-permute-start | bytes 172040 | tf_op jit(solution)/shard_map/ppermute | solution.py:8
  255.9 8.1 %collective-permute-start.14 = (f32[2,3]{1,0:T(2,128)S(1)}, f32[2,3]{1,0:T(2,128)S(1)}, u32[]{:S(2)}, u32[]{:S(2)}) collective-permute-start(f32[2,3]{1,0:T(2,128)S(1)} %reduce_sum.279), channel_id=1, source_target_pairs={{0,16},{16,0},{32,48},{48,32},{64,80},{80,64},{96,112},{112,96},{1... | collective-permute-start | bytes 80 | tf_op jit(solution)/shard_map/ppermute | solution.py:8
  264.2 2.4 collective-permute-start.15
  266.7 2.4 collective-permute-start.16
  269.1 3.9 %collective-permute-start.17 = (f32[2,3]{1,0:T(2,128)S(1)}, f32[2,3]{1,0:T(2,128)S(1)}, u32[]{:S(2)}, u32[]{:S(2)}) collective-permute-start(f32[2,3]{1,0:T(2,128)S(1)} %add.183), channel_id=1, source_target_pairs={{0,128},{16,144},{32,160},{48,176},{64,192},{80,208},{96,224},{112... | collective-permute-start | bytes 80 | tf_op jit(solution)/shard_map/ppermute | solution.py:8
  278.9 46.2 %copy-start.7 = (f32[256,512]{1,0:T(8,128)S(1)}, f32[256,512]{1,0:T(8,128)}, u32[]{:S(2)}) copy-start(f32[256,512]{1,0:T(8,128)} %param.15) | copy-start | bytes 1572868
  304.1 21.1 %copy-start.6 = (f32[256,512]{1,0:T(8,128)S(1)}, f32[256,512]{1,0:T(8,128)}, u32[]{:S(2)}) copy-start(f32[256,512]{1,0:T(8,128)} %param.14) | copy-start | bytes 1572868
  304.1 21.1 %copy-start.5 = (f32[256,512]{1,0:T(8,128)S(1)}, f32[256,512]{1,0:T(8,128)}, u32[]{:S(2)}) copy-start(f32[256,512]{1,0:T(8,128)} %param.13) | copy-start | bytes 1572868
  325.1 1.5 copy-start.2
  325.1 2.0 copy-start.3
  325.2 2.3 copy-start.4
